TPU v7x, 32 devices: a whole 2x2x4 slice. The times are simulated.
32 devices in a mesh: grp: 4 (over z), cp: 8 (over y, x, core).
Axes of the slice: x: 2, y: 2, z: 4, core: 2. Of those that a mesh axis runs over, the one named last changes fastest.
Arguments:
- query: bfloat16 [8192, 2048], P(('grp', 'cp')), may hold values from -6 to 6
- key: bfloat16 [8192, 512], P(('grp', 'cp')), may hold values from -6 to 6
- value: bfloat16 [8192, 512], P(('grp', 'cp')), may hold values from -6 to 6
- output_gradient: bfloat16 [8192, 2048], P(('grp', 'cp')), may hold values from -0.59765625 to 0.59765625
- lse: bfloat16 [8192, 16], P(('grp', 'cp')), may hold values from 1 to 3
- delta: bfloat16 [8192, 16], P(('grp', 'cp')), may hold values from -6 to 6
- lengths: int32 [4], replicated, may hold values from 1 to 4096, as said below
- plan: int32 [512], P(('grp', 'cp')), may hold values from -1 to 6, as said below
Outputs:
- dquery: bfloat16 [8192, 2048], P(('grp', 'cp'))
- dkey: bfloat16 [8192, 512], P(('grp', 'cp'))
- dvalue: bfloat16 [8192, 512], P(('grp', 'cp'))
Inputs may be any that keep to these rules, and one draw needn't show every extreme that they name: `lengths`: in order; they sum to 8192, and the longest is 4096. `plan`: a block's entry is -1 or a member index of its own group below the member that holds the block, whose shard holds tokens of the document of the block's first row; the blocks of one device name distinct members.
All inputs are finite; a program needn't handle non-finite values.
Results may differ from a plain program's by a relative error of at most 0.0061.
Values may be sent and summed in bfloat16 or wider, within the bound.
A program may use at most 128 MiB of HBM per device.

v0:
```python
import jax
import jax.numpy as jnp
from jax import lax
from jax.sharding import PartitionSpec as P

QUERY_HEADS = 16
KEY_VALUE_HEADS = 4
HEAD_SIZE = 128


def shifted_2(value, axis, steps):
    count = lax.axis_size(axis)
    first, last = (max(0, -steps), min(count, count - steps))
    return lax.ppermute(value, axis, [(source, source + steps) for source in range(first, last)])


def doc_ids(position, doc_ends):
    return jnp.sum((doc_ends[None, :] <= position[:, None]).astype(jnp.int32), axis=1)


def head_grads(queries, grad_rows, lse_rows, delta_rows, keys_head, values_head, allowed):
    factor = HEAD_SIZE ** (-0.5)
    score_matrix = (
        jnp.einsum("rgd,cd->rgc", queries, keys_head, preferred_element_type=jnp.float32) * factor
    )
    shifted = jnp.where(allowed[:, None, :], score_matrix - lse_rows[:, :, None], -jnp.inf)
    probs = jnp.exp(shifted)
    dprobs = jnp.einsum("rgd,cd->rgc", grad_rows, values_head, preferred_element_type=jnp.float32)
    dscores = probs * (dprobs - delta_rows[:, :, None])
    probs_low = probs.astype(jnp.bfloat16)
    dscores_low = dscores.astype(jnp.bfloat16)
    value_gradient = jnp.einsum(
        "rgc,rgd->cd", probs_low, grad_rows, preferred_element_type=jnp.float32
    )
    key_gradient = (
        jnp.einsum("rgc,rgd->cd", dscores_low, queries, preferred_element_type=jnp.float32) * factor
    )
    grad_query = (
        jnp.einsum("rgc,cd->rgd", dscores_low, keys_head, preferred_element_type=jnp.float32)
        * factor
    )
    return (grad_query, key_gradient, value_gradient)


def attention_grads(query, output_gradient, lse, delta, key, value, allowed):
    query_count = query.shape[0]
    key_count = key.shape[0]
    query_group = QUERY_HEADS // KEY_VALUE_HEADS
    query_per_head = jnp.moveaxis(
        query.reshape(query_count, KEY_VALUE_HEADS, query_group, HEAD_SIZE), 1, 0
    )
    gradient_per_head = jnp.moveaxis(
        output_gradient.reshape(query_count, KEY_VALUE_HEADS, query_group, HEAD_SIZE), 1, 0
    )
    logsumexp_per_head = jnp.moveaxis(
        lse.astype(jnp.float32).reshape(query_count, KEY_VALUE_HEADS, query_group), 1, 0
    )
    delta_per_head = jnp.moveaxis(
        delta.astype(jnp.float32).reshape(query_count, KEY_VALUE_HEADS, query_group), 1, 0
    )
    key_per_head = jnp.moveaxis(key.reshape(key_count, KEY_VALUE_HEADS, HEAD_SIZE), 1, 0)
    value_per_head = jnp.moveaxis(value.reshape(key_count, KEY_VALUE_HEADS, HEAD_SIZE), 1, 0)

    def per_head(pieces):
        return head_grads(pieces[0], pieces[1], pieces[2], pieces[3], pieces[4], pieces[5], allowed)

    grad_query, key_gradient, value_gradient = lax.map(
        per_head,
        (
            query_per_head,
            gradient_per_head,
            logsumexp_per_head,
            delta_per_head,
            key_per_head,
            value_per_head,
        ),
    )
    return (
        jnp.moveaxis(grad_query, 0, 1).reshape(query_count, QUERY_HEADS * HEAD_SIZE),
        jnp.moveaxis(key_gradient, 0, 1).reshape(key_count, KEY_VALUE_HEADS * HEAD_SIZE),
        jnp.moveaxis(value_gradient, 0, 1).reshape(key_count, KEY_VALUE_HEADS * HEAD_SIZE),
    )


def routed_grads(
    slot_query,
    slot_grad,
    slot_lse,
    slot_delta,
    slot_pos,
    slot_valid,
    key,
    value,
    key_pos,
    key_doc,
    doc_ends,
):
    position = slot_pos.reshape(-1)
    live_rows = jnp.broadcast_to(slot_valid[:, None], slot_pos.shape).reshape(-1)
    query_doc = doc_ids(position, doc_ends)
    allowed = (
        live_rows[:, None]
        & (query_doc[:, None] == key_doc[None, :])
        & (key_pos[None, :] <= position[:, None])
    )
    width_q = QUERY_HEADS * HEAD_SIZE
    return attention_grads(
        slot_query.reshape(-1, width_q),
        slot_grad.reshape(-1, width_q),
        slot_lse.reshape(-1, QUERY_HEADS),
        slot_delta.reshape(-1, QUERY_HEADS),
        key,
        value,
        allowed,
    )


def on_device(query, key, value, output_gradient, lse, delta, lengths, plan):
    local_rows = query.shape[0]
    members = lax.axis_size("cp")
    shard_id = lax.axis_index(("grp", "cp"))
    group_member = lax.axis_index("cp")
    doc_ends = jnp.cumsum(lengths)
    offsets = jnp.arange(local_rows, dtype=jnp.int32)
    position = shard_id * local_rows + offsets
    own_doc = doc_ids(position, doc_ends)
    blocks = plan.shape[0]
    block_rows = local_rows // blocks
    group_plan = lax.all_gather(plan, "cp", axis=0, tiled=True).reshape(members, blocks)
    earlier = shifted_2((key, value), ("grp", "cp"), 1)
    key_rows = jnp.concatenate([earlier[0], key], axis=0)
    value_rows = jnp.concatenate([earlier[1], value], axis=0)
    key_pos = shard_id * local_rows - local_rows + jnp.arange(2 * local_rows, dtype=jnp.int32)
    key_doc = doc_ids(key_pos, doc_ends)
    skip_prev = (jnp.repeat(plan, block_rows) == group_member - 1) & (group_member >= 1)
    allowed_pair = (
        (own_doc[:, None] == key_doc[None, :])
        & (key_pos[None, :] <= position[:, None])
        & (key_pos[None, :] >= 0)
    )
    allowed_pair = allowed_pair & jnp.logical_not(
        skip_prev[:, None] & (key_pos[None, :] < shard_id * local_rows)
    )
    grad_query, dk_pair, dv_pair = attention_grads(
        query, output_gradient, lse, delta, key_rows, value_rows, allowed_pair
    )
    returned_gradients = shifted_2((dk_pair[:local_rows], dv_pair[:local_rows]), ("grp", "cp"), -1)
    key_gradient = dk_pair[local_rows:] + returned_gradients[0]
    value_gradient = dv_pair[local_rows:] + returned_gradients[1]
    width_q = QUERY_HEADS * HEAD_SIZE
    peer_ids = jnp.arange(members, dtype=jnp.int32)
    select = plan[None, :] == peer_ids[:, None]
    select_low = select.astype(jnp.bfloat16)

    def to_slots(source):
        return jnp.dot(
            select_low, source.reshape(blocks, -1), preferred_element_type=jnp.float32
        ).astype(jnp.bfloat16)

    incoming = (
        lax.all_to_all(to_slots(query), "cp", split_axis=0, concat_axis=0, tiled=True),
        lax.all_to_all(to_slots(output_gradient), "cp", split_axis=0, concat_axis=0, tiled=True),
        lax.all_to_all(to_slots(lse), "cp", split_axis=0, concat_axis=0, tiled=True),
        lax.all_to_all(to_slots(delta), "cp", split_axis=0, concat_axis=0, tiled=True),
    )
    slot_hits = group_plan == group_member
    slot_valid = jnp.any(slot_hits, axis=1)
    block_index = jnp.sum(
        slot_hits.astype(jnp.int32) * jnp.arange(blocks, dtype=jnp.int32)[None, :], axis=1
    )
    sender_shard = shard_id - group_member + peer_ids
    slot_pos = (sender_shard * local_rows + block_index * block_rows)[:, None] + jnp.arange(
        block_rows, dtype=jnp.int32
    )[None, :]
    dq_routed, dk_routed, dv_routed = routed_grads(
        incoming[0],
        incoming[1],
        incoming[2],
        incoming[3],
        slot_pos,
        slot_valid,
        key,
        value,
        position,
        own_doc,
        doc_ends,
    )
    dq_slots = dq_routed.reshape(members, -1)
    returned_dq = lax.all_to_all(dq_slots, "cp", split_axis=0, concat_axis=0, tiled=True)
    dq_home = jnp.dot(select.astype(jnp.float32).T, returned_dq, precision=lax.Precision.HIGHEST)
    grad_query = grad_query + dq_home.reshape(local_rows, width_q)
    return (
        grad_query.astype(jnp.bfloat16),
        (key_gradient + dk_routed).astype(jnp.bfloat16),
        (value_gradient + dv_routed).astype(jnp.bfloat16),
    )


def solution(mesh):
    placed = (
        P(("grp", "cp"), None),
        P(("grp", "cp"), None),
        P(("grp", "cp"), None),
        P(("grp", "cp"), None),
        P(("grp", "cp"), None),
        P(("grp", "cp"), None),
        P(),
        P(("grp", "cp")),
    )
    return jax.shard_map(
        on_device,
        mesh=mesh,
        in_specs=placed,
        out_specs=(P(("grp", "cp"), None), P(("grp", "cp"), None), P(("grp", "cp"), None)),
        check_vma=False,
    )
```

profile of v0, /device:TPU:11, one launch (start us, length us, event | category | flops | bytes accessed | tf_op | source)
XLA Modules:
  0.0 153.1 jit_solution(9783688158153302052)
XLA Ops:
  1.7 3.7 %collective-permute-start = (bf16[256,512]{0,1:T(8,128)(2,1)S(1)}, bf16[256,512]{0,1:T(8,128)(2,1)}, u32[]{:S(2)}, u32[]{:S(2)}) collective-permute-start(bf16[256,512]{0,1:T(8,128)(2,1)S(1)} %copy.137), channel_id=1, source_target_pairs={{0,1},{1,2},{2,3},{3,4},{4,5},{5,6},{6,7},{7,8},{8,9},{9,10},{10,1... | collective-permute-start | bytes 786440 | tf_op jit(solution)/shard_map/ppermute | solution.py:14
  5.4 1.8 %copy.140 = bf16[256,512]{0,1:T(8,128)(2,1)} copy(bf16[256,512]{1,0:T(8,128)(2,1)} %param.14) | data formatting | bytes 524288 | tf_op args[2]
  7.2 2.0 %collective-permute-start.1 = (bf16[256,512]{0,1:T(8,128)(2,1)}, bf16[256,512]{0,1:T(8,128)(2,1)}, u32[]{:S(2)}, u32[]{:S(2)}) collective-permute-start(bf16[256,512]{0,1:T(8,128)(2,1)} %copy.140), channel_id=1, source_target_pairs={{0,1},{1,2},{2,3},{3,4},{4,5},{5,6},{6,7},{7,8},{8,9},{9,10},{10,1... | collective-permute-start | bytes 786440 | tf_op jit(solution)/shard_map/ppermute | solution.py:14
  12.8 4.4 %all-to-all-start.1 = ((bf16[8,2,128]{2,1,0:T(2,128)(2,1)}), bf16[8,2,128]{2,1,0:T(2,128)(2,1)S(1)}, u32[]{:S(2)}, u32[]{:S(2)}) async-start(bf16[8,2,128]{2,1,0:T(2,128)(2,1)} %reshape.230), calls=%async_computation.1 | async-start | bytes 8192 | tf_op jit(solution)/shard_map/all_to_all | solution.py:163
  20.9 5.3 %all-reduce = s32[128]{0:T(128)S(1)} all-reduce(s32[128]{0:T(128)S(1)} %dynamic-update-slice), channel_id=1, replica_groups=mesh['grp'=4,'cp'=8] {'cp'}, use_global_device_ids=true, to_apply=%add | all-reduce | flops 128 | bytes 1024
  26.7 1.6 %reshape.198 = bf16[16,32768]{1,0:T(8,128)(2,1)S(1)} reshape(bf16[256,2048]{1,0:T(8,128)(2,1)} %param.12) | data formatting | bytes 2097152 | tf_op jit(solution)/shard_map/reshape | solution.py:157
  32.6 6.4 %all-to-all-start.3 = ((bf16[8,2,128]{2,1,0:T(2,128)(2,1)}), bf16[8,2,128]{2,1,0:T(2,128)(2,1)S(1)}, u32[]{:S(2)}, u32[]{:S(2)}) async-start(bf16[8,2,128]{2,1,0:T(2,128)(2,1)} %reshape.234), calls=%async_computation.3 | async-start | bytes 8192 | tf_op jit(solution)/shard_map/all_to_all | solution.py:164
  40.7 2.0 %reduce.6 = bf16[8,32768]{1,0:T(8,128)(2,1)S(1)} reduce(bf16[8,1,32768]{2,0,1:T(8,128)(2,1)} %fusion.53, bf16[]{:T(256)} %broadcast.132), dimensions={1}, to_apply=%copy.147.reduce_sub_computation | reduce | bytes 1048578 | tf_op jit(solution)/shard_map/all_to_all | solution.py:161
  46.1 4.2 %all-to-all-start = ((bf16[8,2,16384]{2,1,0:T(2,128)(2,1)}), bf16[8,2,16384]{2,1,0:T(2,128)(2,1)}, u32[]{:S(2)}, u32[]{:S(2)}) async-start(bf16[8,2,16384]{2,1,0:T(2,128)(2,1)} %reshape.228), calls=%async_computation | async-start | bytes 1048576 | tf_op jit(solution)/shard_map/all_to_all | solution.py:161
  53.4 5.2 %all-to-all-done = bf16[8,2,16384]{2,1,0:T(2,128)(2,1)} async-done(((bf16[8,2,16384]{2,1,0:T(2,128)(2,1)}), bf16[8,2,16384]{2,1,0:T(2,128)(2,1)}, u32[]{:S(2)}, u32[]{:S(2)}) %all-to-all-start) | async-done | bytes 524320 | tf_op jit(solution)/shard_map/all_to_all | solution.py:161
  58.6 5.5 %all-to-all-start.2 = ((bf16[8,2,16384]{2,1,0:T(2,128)(2,1)}), bf16[8,2,16384]{2,1,0:T(2,128)(2,1)}, u32[]{:S(2)}, u32[]{:S(2)}) async-start(bf16[8,2,16384]{2,1,0:T(2,128)(2,1)} %reshape.232), calls=%async_computation.2 | async-start | bytes 1048576 | tf_op jit(solution)/shard_map/all_to_all | solution.py:162
  64.2 20.1 %while.30 = (s32[]{:T(128)}, f32[4,256,4,128]{3,1,2,0:T(8,128)}, f32[4,512,128]{2,1,0:T(8,128)}, f32[4,512,128]{2,1,0:T(8,128)}, bf16[4,256,4,128]{1,3,2,0:T(8,1...) while((s32[]{:T(128)}, f32[4,256,4,128]{3,1,2,0:T(8,128)}, ...), condition=%wide.region_4.5_spmd.clone, body=%wide.region_3.4_spmd.clone.sunk | while | flops 675872768 | bytes 12226985 | solution.py:67
  75.6 1.3 fusion.114
  80.7 1.3 fusion.114
  84.3 2.1 %slice_bitcast_fusion.1 = (f32[4,32,8,128]{3,2,1,0:T(8,128)}, f32[4,32,8,128]{3,2,1,0:T(8,128)S(1)}) fusion(f32[512,4,128]{2,0,1:T(8,128)} %bitcast.30), kind=kLoop, calls=%fused_computation.92 | loop fusion | bytes 2097152
  87.3 2.5 %collective-permute-start.3 = (f32[256,512]{1,0:T(8,128)}, f32[256,512]{1,0:T(8,128)}, u32[]{:S(2)}, u32[]{:S(2)}) collective-permute-start(f32[256,512]{1,0:T(8,128)} %bitcast.189), channel_id=1, source_target_pairs={{1,0},{2,1},{3,2},{4,3},{5,4},{6,5},{7,6},{8,7},{9,8},{10,9},{11,1... | collective-permute-start | bytes 1572872 | tf_op jit(solution)/shard_map/ppermute | solution.py:14
  89.7 2.2 %reshape.229 = bf16[8,1,32768]{2,1,0:T(2,128)(2,1)S(1)} reshape(bf16[8,2,16384]{2,1,0:T(2,128)(2,1)} %all-to-all-done) | data formatting | bytes 1048576
  92.0 3.2 %reduce = bf16[8,32768]{1,0:T(8,128)(2,1)S(1)} reduce(bf16[8,1,32768]{2,1,0:T(2,128)(2,1)S(1)} %reshape.229, bf16[]{:T(256)} %constant.92), dimensions={1}, to_apply=%all_to_all.33.reduce_sub_computation | reduce | bytes 1048578 | tf_op jit(solution)/shard_map/all_to_all | solution.py:161
  95.5 2.3 %reshape.233 = bf16[8,1,32768]{2,1,0:T(2,128)(2,1)S(1)} reshape(bf16[8,2,16384]{2,1,0:T(2,128)(2,1)} %all-to-all-done.2) | data formatting | bytes 1048576
  97.8 3.2 %reduce.2 = bf16[8,32768]{1,0:T(8,128)(2,1)S(1)} reduce(bf16[8,1,32768]{2,1,0:T(2,128)(2,1)S(1)} %reshape.233, bf16[]{:T(256)} %constant.92), dimensions={1}, to_apply=%all_to_all.37.reduce_sub_computation | reduce | bytes 1048578 | tf_op jit(solution)/shard_map/all_to_all | solution.py:162
  101.4 14.6 %while.31 = (s32[]{:T(128)}, f32[4,128,4,128]{3,1,2,0:T(8,128)S(1)}, f32[4,256,128]{2,1,0:T(8,128)}, f32[4,256,128]{2,1,0:T(8,128)}, bf16[4,128,4,128]{3,2,0,1:T...) while((s32[]{:T(128)}, ...), condition=%wide.region_9.10_spmd.clone, body=%wide.region_8.9_spmd.clone.sunk | while | flops 168919040 | bytes 4212513 | solution.py:67
  116.0 1.7 %copy.161 = f32[128,4,4,128]{3,2,1,0:T(4,128)} copy(f32[128,4,4,128]{3,0,2,1:T(8,128)S(1)} %bitcast.255) | data formatting | bytes 2097152 | tf_op jit(solution)/shard_map/transpose | solution.py:79
  117.7 5.9 %all-to-all-start.4 = ((f32[8,1,32768]{2,1,0:T(1,128)}), f32[8,1,32768]{2,1,0:T(1,128)S(1)}, u32[]{:S(2)}, u32[]{:S(2)}) async-start(f32[8,1,32768]{2,1,0:T(1,128)} %bitcast.27), calls=%async_computation.4 | async-start | bytes 2097152 | tf_op jit(solution)/shard_map/all_to_all | solution.py:189
  125.3 2.5 %collective-permute-start.2 = (f32[256,512]{1,0:T(8,128)}, f32[256,512]{1,0:T(8,128)}, u32[]{:S(2)}, u32[]{:S(2)}) collective-permute-start(f32[256,512]{1,0:T(8,128)} %bitcast.190), channel_id=1, source_target_pairs={{1,0},{2,1},{3,2},{4,3},{5,4},{6,5},{7,6},{8,7},{9,8},{10,9},{11,1... | collective-permute-start | bytes 1572872 | tf_op jit(solution)/shard_map/ppermute | solution.py:14
  127.8 2.7 %copy.146 = f32[256,4,4,128]{3,2,1,0:T(4,128)} copy(f32[256,4,4,128]{3,0,2,1:T(8,128)S(1)} %bitcast.254) | data formatting | bytes 4194304 | tf_op jit(solution)/shard_map/transpose | solution.py:79
  130.5 2.1 %reshape.197 = f32[256,2048]{1,0:T(8,128)S(1)} reshape(f32[256,4,4,128]{3,2,1,0:T(4,128)} %copy.146) | data formatting | bytes 4194304 | tf_op jit(solution)/shard_map/reshape | solution.py:79
  132.7 2.2 %fusion.60 = bf16[256,512]{1,0:T(8,128)(2,1)} fusion(f32[256,512]{1,0:T(8,128)} %collective-permute-done.3, f32[4,32,8,128]{3,2,1,0:T(8,128)} %get-tuple-element.405, f32[4,256,128]{2,1,0:T(8,128)} %get-tuple-element.126), kind=kLoop, calls=%fused_computation.84 | loop fusion | flops 393216 | bytes 1835008 | tf_op jit(solution)/shard_map/convert_element_type | solution.py:195
  134.9 8.1 %collective-permute-done.2 = f32[256,512]{1,0:T(8,128)} collective-permute-done((f32[256,512]{1,0:T(8,128)}, f32[256,512]{1,0:T(8,128)}, u32[]{:S(2)}, u32[]{:S(2)}) %collective-permute-start.2) | collective-permute-done | bytes 524320 | tf_op jit(solution)/shard_map/ppermute | solution.py:14
  143.0 1.8 %fusion.61 = bf16[256,512]{1,0:T(8,128)(2,1)} fusion(f32[256,512]{1,0:T(8,128)} %collective-permute-done.2, f32[4,32,8,128]{3,2,1,0:T(8,128)S(1)} %copy-done.4, f32[4,256,128]{2,1,0:T(8,128)S(1)} %copy-done.7), kind=kLoop, calls=%fused_computation.88 | loop fusion | flops 393216 | bytes 1835008 | tf_op jit(solution)/shard_map/convert_element_type | solution.py:194
  144.8 2.8 %fusion.57 = f32[16,32768]{1,0:T(8,128)} fusion(f32[8,1,32768]{2,1,0:T(1,128)S(1)} %all-to-all-done.4, s32[16]{0:T(128)S(1)} %copy-done.10), kind=kOutput, calls=%fused_computation.80 | convolution fusion | flops 50331776 | bytes 3145792 | tf_op jit(solution)/shard_map/dot_general | solution.py:190
  147.6 2.7 %reshape.204 = f32[256,2048]{1,0:T(8,128)} reshape(f32[16,32768]{1,0:T(8,128)} %fusion.57) | data formatting | bytes 4194304 | tf_op jit(solution)/shard_map/reshape | solution.py:191
  150.3 2.8 %add_convert_fusion = bf16[256,2048]{1,0:T(8,128)(2,1)} fusion(f32[256,2048]{1,0:T(8,128)S(1)} %reshape.197, f32[256,2048]{1,0:T(8,128)} %reshape.204), kind=kLoop, calls=%fused_computation.75 | loop fusion | flops 1048576 | bytes 5242880 | tf_op jit(solution)/shard_map/convert_element_type | solution.py:193
  (152 shorter events, 55.8 us)
Async XLA Ops:
  0.6 27.6 %copy-start.10 = (s32[16]{0:T(128)S(1)}, s32[16]{0:T(128)}, u32[]{:S(2)}) copy-start(s32[16]{0:T(128)} %param.19) | copy-start | bytes 196
  1.7 49.6 %collective-permute-start = (bf16[256,512]{0,1:T(8,128)(2,1)S(1)}, bf16[256,512]{0,1:T(8,128)(2,1)}, u32[]{:S(2)}, u32[]{:S(2)}) collective-permute-start(bf16[256,512]{0,1:T(8,128)(2,1)S(1)} %copy.137), channel_id=1, source_target_pairs={{0,1},{1,2},{2,3},{3,4},{4,5},{5,6},{6,7},{7,8},{8,9},{9,10},{10,1... | collective-permute-start | bytes 786440 | tf_op jit(solution)/shard_map/ppermute | solution.py:14
  7.2 22.1 %copy-start.1 = (bf16[256,2048]{1,0:T(8,128)(2,1)S(1)}, bf16[256,2048]{1,0:T(8,128)(2,1)}, u32[]{:S(2)}) copy-start(bf16[256,2048]{1,0:T(8,128)(2,1)} %param.15) | copy-start | bytes 3145732
  7.2 45.1 %collective-permute-start.1 = (bf16[256,512]{0,1:T(8,128)(2,1)}, bf16[256,512]{0,1:T(8,128)(2,1)}, u32[]{:S(2)}, u32[]{:S(2)}) collective-permute-start(bf16[256,512]{0,1:T(8,128)(2,1)} %copy.140), channel_id=1, source_target_pairs={{0,1},{1,2},{2,3},{3,4},{4,5},{5,6},{6,7},{7,8},{8,9},{9,10},{10,1... | collective-permute-start | bytes 786440 | tf_op jit(solution)/shard_map/ppermute | solution.py:14
  12.8 19.8 %all-to-all-start.1 = ((bf16[8,2,128]{2,1,0:T(2,128)(2,1)}), bf16[8,2,128]{2,1,0:T(2,128)(2,1)S(1)}, u32[]{:S(2)}, u32[]{:S(2)}) async-start(bf16[8,2,128]{2,1,0:T(2,128)(2,1)} %reshape.230), calls=%async_computation.1 | async-start | bytes 8192 | tf_op jit(solution)/shard_map/all_to_all | solution.py:163
  29.3 1.6 %copy-start.9 = (bf16[256,16]{0,1:T(8,128)(2,1)S(1)}, bf16[256,16]{0,1:T(8,128)(2,1)}, u32[]{:S(2)}) copy-start(bf16[256,16]{0,1:T(8,128)(2,1)} %param.17) | copy-start | bytes 24580
  29.3 9.7 %copy-start = (bf16[256,2048]{1,0:T(8,128)(2,1)S(1)}, bf16[256,2048]{1,0:T(8,128)(2,1)}, u32[]{:S(2)}) copy-start(bf16[256,2048]{1,0:T(8,128)(2,1)} %param.12) | copy-start | bytes 3145732
  32.6 13.5 %all-to-all-start.3 = ((bf16[8,2,128]{2,1,0:T(2,128)(2,1)}), bf16[8,2,128]{2,1,0:T(2,128)(2,1)S(1)}, u32[]{:S(2)}, u32[]{:S(2)}) async-start(bf16[8,2,128]{2,1,0:T(2,128)(2,1)} %reshape.234), calls=%async_computation.3 | async-start | bytes 8192 | tf_op jit(solution)/shard_map/all_to_all | solution.py:164
  39.0 1.1 copy-start.8
  40.1 3.8 %copy-start.3 = (bf16[8,1,32768]{2,0,1:T(8,128)(2,1)S(1)}, bf16[8,1,32768]{2,0,1:T(8,128)(2,1)}, u32[]{:S(2)}) copy-start(bf16[8,1,32768]{2,0,1:T(8,128)(2,1)} %fusion.54) | copy-start | bytes 1572868
  46.1 12.5 %all-to-all-start = ((bf16[8,2,16384]{2,1,0:T(2,128)(2,1)}), bf16[8,2,16384]{2,1,0:T(2,128)(2,1)}, u32[]{:S(2)}, u32[]{:S(2)}) async-start(bf16[8,2,16384]{2,1,0:T(2,128)(2,1)} %reshape.228), calls=%async_computation | async-start | bytes 1048576 | tf_op jit(solution)/shard_map/all_to_all | solution.py:161
  58.6 36.9 %all-to-all-start.2 = ((bf16[8,2,16384]{2,1,0:T(2,128)(2,1)}), bf16[8,2,16384]{2,1,0:T(2,128)(2,1)}, u32[]{:S(2)}, u32[]{:S(2)}) async-start(bf16[8,2,16384]{2,1,0:T(2,128)(2,1)} %reshape.232), calls=%async_computation.2 | async-start | bytes 1048576 | tf_op jit(solution)/shard_map/all_to_all | solution.py:162
  87.3 45.4 %collective-permute-start.3 = (f32[256,512]{1,0:T(8,128)}, f32[256,512]{1,0:T(8,128)}, u32[]{:S(2)}, u32[]{:S(2)}) collective-permute-start(f32[256,512]{1,0:T(8,128)} %bitcast.189), channel_id=1, source_target_pairs={{1,0},{2,1},{3,2},{4,3},{5,4},{6,5},{7,6},{8,7},{9,8},{10,9},{11,1... | collective-permute-start | bytes 1572872 | tf_op jit(solution)/shard_map/ppermute | solution.py:14
  95.5 5.9 %copy-start.5 = (f32[4,128,4,128]{3,1,2,0:T(8,128)S(1)}, f32[4,128,4,128]{3,1,2,0:T(8,128)}, u32[]{:S(2)}) copy-start(f32[4,128,4,128]{3,1,2,0:T(8,128)} %custom-call.3) | copy-start | bytes 3145732
  116.0 7.6 %copy-start.6 = (f32[4,512,128]{2,1,0:T(8,128)S(1)}, f32[4,512,128]{2,1,0:T(8,128)}, u32[]{:S(2)}) copy-start(f32[4,512,128]{2,1,0:T(8,128)} %get-tuple-element.123) | copy-start | bytes 3145732
  117.7 27.1 %all-to-all-start.4 = ((f32[8,1,32768]{2,1,0:T(1,128)}), f32[8,1,32768]{2,1,0:T(1,128)S(1)}, u32[]{:S(2)}, u32[]{:S(2)}) async-start(f32[8,1,32768]{2,1,0:T(1,128)} %bitcast.27), calls=%async_computation.4 | async-start | bytes 2097152 | tf_op jit(solution)/shard_map/all_to_all | solution.py:189
  123.6 4.3 %copy-start.2 = (f32[4,256,4,128]{3,1,2,0:T(8,128)S(1)}, f32[4,256,4,128]{3,1,2,0:T(8,128)}, u32[]{:S(2)}) copy-start(f32[4,256,4,128]{3,1,2,0:T(8,128)} %get-tuple-element.121) | copy-start | bytes 6291460
  125.3 17.7 %collective-permute-start.2 = (f32[256,512]{1,0:T(8,128)}, f32[256,512]{1,0:T(8,128)}, u32[]{:S(2)}, u32[]{:S(2)}) collective-permute-start(f32[256,512]{1,0:T(8,128)} %bitcast.190), channel_id=1, source_target_pairs={{1,0},{2,1},{3,2},{4,3},{5,4},{6,5},{7,6},{8,7},{9,8},{10,9},{11,1... | collective-permute-start | bytes 1572872 | tf_op jit(solution)/shard_map/ppermute | solution.py:14
  132.6 10.3 %copy-start.4 = (f32[4,32,8,128]{3,2,1,0:T(8,128)S(1)}, f32[4,32,8,128]{3,2,1,0:T(8,128)}, u32[]{:S(2)}) copy-start(f32[4,32,8,128]{3,2,1,0:T(8,128)} %get-tuple-element.407) | copy-start | bytes 1572868
  132.6 10.3 %copy-start.7 = (f32[4,256,128]{2,1,0:T(8,128)S(1)}, f32[4,256,128]{2,1,0:T(8,128)}, u32[]{:S(2)}) copy-start(f32[4,256,128]{2,1,0:T(8,128)} %get-tuple-element.124) | copy-start | bytes 1572868
where the time goes:
time: 154 us; the launch traced here: 153 us
  matrix products  38.5 us (25%)
  starting transfers between devices  37.1 us (24%)
  local copies, waits for them, and re-layouts  34.5 us (22%)
  other arithmetic  22.5 us (15%)
  waiting for transfers between devices  13.3 us (9%)
  blocking collectives  5.31 us (3%)
  between operations  1.68 us (1%)
    unnamed x43, local copies, waits for them, and re-layouts  18.3 us
    ppermute x4, starting transfers between devices, shifted_2(): lax.ppermute(value, axis, [(source, source + steps) for source in range(f...  10.7 us
    dot_general x8, matrix products, head_grads(): jnp.einsum('rgc,rgd->cd', probs_low, grad_rows, preferred_element_type=jn...  8.44 us
    dot_general x8, matrix products, head_grads(): jnp.einsum('rgc,rgd->cd', dscores_low, queries, preferred_element_type=jn...  8.39 us
    ppermute x4, waiting for transfers between devices, shifted_2(): lax.ppermute(value, axis, [(source, source + steps) for source in range(f...  8.08 us
    all_to_all x1, starting transfers between devices, on_device(): lax.all_to_all(to_slots(delta), 'cp', split_axis=0, concat_axis=0, tiled=...  6.43 us
    dot_general x8, matrix products, head_grads(): jnp.einsum('rgd,cd->rgc', grad_rows, values_head, preferred_element_type=...  6.16 us
    dot_general x8, matrix products, head_grads(): jnp.einsum('rgc,cd->rgd', dscores_low, keys_head, preferred_element_type=...  5.89 us
  transfers between devices with their start and end apart: 9, of which 2 were waited for; matrix products, arithmetic and copies ran while one was open for 56% of the time, Pallas kernels for 0%

commit v1 on v0

v1 whole, which is shorter than its diff:
```python
import functools
import math

import jax
import jax.numpy as jnp
from jax import lax
from jax.experimental import pallas as pl
from jax.experimental.pallas import tpu as pltpu
from jax.sharding import PartitionSpec as P

HEAD_SIZE = 128
FACTOR = HEAD_SIZE**-0.5
LOG2E = math.log2(math.e)
F32 = jnp.float32
BF16 = jnp.bfloat16
MESH = pl.DeviceIdType.MESH


def dot_nt(a, b):
    return lax.dot_general(a, b, (((1,), (1,)), ((), ())), preferred_element_type=F32)


def dot_nn(a, b):
    return jnp.dot(a, b, preferred_element_type=F32)


def group_grads(queries, grads, lse_rows, delta_rows, keys, values, bias):
    keys_t = keys.T
    probs_low, dscores_low, grad_query = [], [], []
    for q, do, lse, delta in zip(queries, grads, lse_rows, delta_rows):
        scores = dot_nt(keys, q)
        probs = jnp.exp2(scores * (FACTOR * LOG2E) + (bias - lse))
        dscores = probs * (dot_nt(values, do) - delta)
        probs_low.append(probs.astype(BF16))
        dscores_low.append(dscores.astype(BF16))
        grad_query.append(dot_nn(keys_t, dscores_low[-1]))
    dv = dot_nn(jnp.concatenate(probs_low, axis=1), jnp.concatenate(grads, axis=0))
    dk = dot_nn(jnp.concatenate(dscores_low, axis=1), jnp.concatenate(queries, axis=0))
    return grad_query, dk, dv


def kernel(
    n,
    groups,
    lengths,
    plan,
    q_ref,
    do_ref,
    k_ref,
    v_ref,
    lse_ref,
    delta_ref,
    dq_ref,
    dk_ref,
    dv_ref,
    slot_out,
    slot_in,
    stat_out,
    stat_in,
    k_prev,
    v_prev,
    back_out,
    back_in,
    dq_out,
    dq_in,
    pick_t,
    stats_t,
    bias_own,
    bias_prev,
    bias_in,
    routed_t,
    dq_t,
    dq_acc,
    dk_acc,
    dv_acc,
    slot_send,
    slot_recv,
    stat_send,
    stat_recv,
    kv_send,
    kv_recv,
    back_send,
    back_recv,
    dqs_send,
    dqs_recv,
):
    grp = lax.axis_index("grp")
    me = lax.axis_index("cp")
    shard = grp * n + me
    last = groups * n - 1
    rows, width_q = q_ref.shape
    width_k = k_ref.shape[1]
    heads = width_q // HEAD_SIZE
    kv_heads = width_k // HEAD_SIZE
    per = heads // kv_heads
    blocks = plan.shape[0]
    block = rows // blocks
    ndocs = lengths.shape[0]
    base = shard * rows
    right = (jnp.where(me == n - 1, jnp.minimum(grp + 1, groups - 1), grp), lax.rem(me + 1, n))
    left = (jnp.where(me == 0, jnp.maximum(grp - 1, 0), grp), lax.rem(me + n - 1, n))
    cross_right = (me == n - 1) & (grp < groups - 1)
    cross_left = (me == 0) & (grp > 0)
    sends = jnp.maximum(me - 1, 0)

    barrier = pltpu.get_barrier_semaphore()

    def greet(step, carry):
        peer = lax.rem(me + step, n)
        pl.semaphore_signal(barrier, inc=1, device_id=(grp, peer), device_id_type=MESH)
        return carry

    lax.fori_loop(1, n, greet, 0)

    @pl.when(cross_right)
    def _():
        pl.semaphore_signal(barrier, inc=1, device_id=right, device_id_type=MESH)

    @pl.when(cross_left)
    def _():
        pl.semaphore_signal(barrier, inc=1, device_id=left, device_id_type=MESH)

    pos = base + lax.broadcasted_iota(jnp.int32, (8, rows), 1)
    start = jnp.zeros((8, rows), jnp.int32)
    end = jnp.int32(0)
    for d in range(ndocs):
        end = end + lengths[d]
        start = jnp.where(pos >= end, end, start)
    lse_rows = lse_ref[...].astype(F32) * LOG2E
    delta_rows = delta_ref[...].astype(F32)
    pad = HEAD_SIZE - 2 * heads - 16
    packed = jnp.concatenate(
        [
            lse_rows,
            delta_rows,
            start.astype(F32),
            jnp.ones((8, rows), F32),
            jnp.zeros((pad, rows), F32),
        ],
        axis=0,
    )
    stats_t[...] = packed

    count = n * block
    owner = jnp.full((8, rows), -1, jnp.int32)
    token = lax.broadcasted_iota(jnp.int32, (8, rows), 1)
    for b in range(blocks):
        owner = jnp.where((token >= b * block) & (token < (b + 1) * block), plan[b], owner)
    within = lax.rem(token, block)
    slot_row = lax.broadcasted_iota(jnp.int32, (count, rows), 0)
    wanted = owner[:1] * block + within[:1]
    pick = jnp.where((slot_row == wanted) & (owner[:1] >= 0), 1.0, 0.0)
    pick_low = pick.astype(BF16)
    pick_t[...] = pick.T.astype(BF16)
    slot_out[:, :, :width_q] = dot_nn(pick_low, q_ref[...]).astype(BF16).reshape(n, block, width_q)
    slot_out[:, :, width_q:] = dot_nn(pick_low, do_ref[...]).astype(BF16).reshape(n, block, width_q)
    stat_out[...] = jnp.dot(
        pick, packed.T, preferred_element_type=F32, precision=lax.Precision.HIGHEST
    ).reshape(n, block, HEAD_SIZE)

    def blank_in(p, carry):
        slot_in[p] = jnp.zeros(slot_in.shape[1:], BF16)
        stat_in[p] = jnp.zeros(stat_in.shape[1:], F32)
        return carry

    lax.fori_loop(0, jnp.minimum(me + 2, n), blank_in, 0)

    def blank_dq(p, carry):
        dq_in[p] = jnp.zeros(dq_in.shape[1:], BF16)
        return carry

    lax.fori_loop(sends, n, blank_dq, 0)

    @pl.when(shard == 0)
    def _():
        k_prev[...] = jnp.zeros_like(k_prev)
        v_prev[...] = jnp.zeros_like(v_prev)

    @pl.when(shard == last)
    def _():
        back_in[...] = jnp.zeros_like(back_in)

    pl.semaphore_wait(barrier, n - 1 + cross_right.astype(jnp.int32) + cross_left.astype(jnp.int32))

    def kv_copies():
        return (
            pltpu.make_async_remote_copy(
                k_ref, k_prev, kv_send.at[0], kv_recv.at[0], device_id=right, device_id_type=MESH
            ),
            pltpu.make_async_remote_copy(
                v_ref, v_prev, kv_send.at[1], kv_recv.at[1], device_id=right, device_id_type=MESH
            ),
        )

    def slot_copies(p, src):
        return (
            pltpu.make_async_remote_copy(
                slot_out.at[p],
                slot_in.at[src],
                slot_send.at[p],
                slot_recv.at[src],
                device_id=(grp, p),
                device_id_type=MESH,
            ),
            pltpu.make_async_remote_copy(
                stat_out.at[p],
                stat_in.at[src],
                stat_send.at[p],
                stat_recv.at[src],
                device_id=(grp, p),
                device_id_type=MESH,
            ),
        )

    def dq_copy(m, src):
        return pltpu.make_async_remote_copy(
            dq_out.at[m],
            dq_in.at[src],
            dqs_send.at[m],
            dqs_recv.at[src],
            device_id=(grp, m),
            device_id_type=MESH,
        )

    def back_copy(g):
        return pltpu.make_async_remote_copy(
            back_out.at[g],
            back_in.at[g],
            back_send.at[g],
            back_recv.at[g],
            device_id=left,
            device_id_type=MESH,
        )

    @pl.when(shard < last)
    def _():
        for copy in kv_copies():
            copy.start()

    def send(p, carry):
        for copy in slot_copies(p, me):
            copy.start()
        return carry

    lax.fori_loop(0, sends, send, 0)

    key_at = lax.broadcasted_iota(jnp.int32, (rows, rows), 0)
    query_at = lax.broadcasted_iota(jnp.int32, (rows, rows), 1)
    begin = start[:1] - base
    bias_own[...] = jnp.where((key_at <= query_at) & (key_at >= begin), 0.0, -jnp.inf)
    bias_prev[...] = jnp.where(key_at - rows >= begin, 0.0, -jnp.inf)

    def columns(h):
        return pl.ds(pl.multiple_of(h * HEAD_SIZE, HEAD_SIZE), HEAD_SIZE)

    def local_inputs(g):
        hs = [g * per + u for u in range(per)]
        return (
            [q_ref[:, columns(h)] for h in hs],
            [do_ref[:, columns(h)] for h in hs],
            [stats_t[pl.ds(h, 1), :] for h in hs],
            [stats_t[pl.ds(heads + h, 1), :] for h in hs],
        )

    def own(g, carry):
        cols = columns(g)
        grad_query, dk, dv = group_grads(
            *local_inputs(g), k_ref[:, cols], v_ref[:, cols], bias_own[...]
        )
        for u in range(per):
            dq_t[columns(g * per + u), :] = grad_query[u]
        dk_acc[:, cols] = dk
        dv_acc[:, cols] = dv
        return carry

    lax.fori_loop(0, kv_heads, own, 0)

    @pl.when(shard > 0)
    def _():
        for copy in kv_copies():
            copy.wait_recv()

    def prev(g, carry):
        cols = columns(g)
        grad_query, dk, dv = group_grads(
            *local_inputs(g), k_prev[:, cols], v_prev[:, cols], bias_prev[...]
        )
        for u in range(per):
            where = columns(g * per + u)
            dq_acc[:, where] = ((dq_t[where, :] + grad_query[u]) * FACTOR).T
        back_out[g, 0] = (dk * FACTOR).astype(BF16)
        back_out[g, 1] = dv.astype(BF16)

        @pl.when(shard > 0)
        def _():
            back_copy(g).start()

        return carry

    lax.fori_loop(0, kv_heads, prev, 0)

    def arrive(m, carry):
        for copy in slot_copies(m, m):
            copy.wait_recv()
        return carry

    lax.fori_loop(me + 2, n, arrive, 0)

    @pl.when(me + 2 < n)
    def _():
        routed_t[...] = stat_in[...].reshape(count, HEAD_SIZE).T
        key_pos = base + lax.broadcasted_iota(jnp.int32, (rows, count), 0)
        first = routed_t[pl.ds(2 * heads, 1), :]
        live = routed_t[pl.ds(2 * heads + 8, 1), :] > 0.5
        bias_in[...] = jnp.where((key_pos.astype(F32) >= first) & live, 0.0, -jnp.inf)

        def routed(g, carry):
            cols = columns(g)
            hs = [g * per + u for u in range(per)]
            grad_query, dk, dv = group_grads(
                [slot_in[:, :, columns(h)].reshape(count, HEAD_SIZE) for h in hs],
                [slot_in[:, :, columns(heads + h)].reshape(count, HEAD_SIZE) for h in hs],
                [routed_t[pl.ds(h, 1), :] for h in hs],
                [routed_t[pl.ds(heads + h, 1), :] for h in hs],
                k_ref[:, cols],
                v_ref[:, cols],
                bias_in[...],
            )
            for u in range(per):
                dq_out[:, :, columns(hs[u])] = (
                    (grad_query[u] * FACTOR).T.astype(BF16).reshape(n, block, HEAD_SIZE)
                )
            dk_acc[:, cols] += dk
            dv_acc[:, cols] += dv
            return carry

        lax.fori_loop(0, kv_heads, routed, 0)

        def give_back(m, carry):
            dq_copy(m, me).start()
            return carry

        lax.fori_loop(me + 2, n, give_back, 0)

    for g in range(kv_heads):

        @pl.when(shard < last)
        def _(g=g):
            back_copy(g).wait_recv()

        cols = pl.ds(g * HEAD_SIZE, HEAD_SIZE)
        dk_ref[:, cols] = (dk_acc[:, cols] * FACTOR + back_in[g, 0].astype(F32)).astype(BF16)
        dv_ref[:, cols] = (dv_acc[:, cols] + back_in[g, 1].astype(F32)).astype(BF16)

    def take(p, carry):
        dq_copy(p, p).wait_recv()
        return carry

    lax.fori_loop(0, sends, take, 0)

    def finish(h, carry):
        cols = columns(h)
        extra = dot_nn(pick_t[...], dq_in[:, :, cols].reshape(count, HEAD_SIZE))
        dq_ref[:, cols] = (dq_acc[:, cols] + extra).astype(BF16)
        return carry

    lax.fori_loop(0, heads, finish, 0)

    @pl.when(shard < last)
    def _():
        for copy in kv_copies():
            copy.wait_send()

    @pl.when(shard > 0)
    def _():
        for g in range(kv_heads):
            back_copy(g).wait_send()

    def sent(p, carry):
        for copy in slot_copies(p, me):
            copy.wait_send()
        return carry

    lax.fori_loop(0, sends, sent, 0)

    def sent_back(m, carry):
        dq_copy(m, me).wait_send()
        return carry

    lax.fori_loop(me + 2, n, sent_back, 0)


def on_device(query, key, value, output_gradient, lse, delta, lengths, plan):
    n = lax.axis_size("cp")
    groups = lax.axis_size("grp")
    rows, width_q = query.shape
    width_k = key.shape[1]
    kv_heads = width_k // HEAD_SIZE
    block = rows // plan.shape[0]
    vmem = pl.BlockSpec(memory_space=pltpu.VMEM)
    smem = pl.BlockSpec(memory_space=pltpu.SMEM)
    dma = pltpu.SemaphoreType.DMA
    return pl.pallas_call(
        functools.partial(kernel, n, groups),
        out_shape=(
            jax.ShapeDtypeStruct((rows, width_q), BF16),
            jax.ShapeDtypeStruct((rows, width_k), BF16),
            jax.ShapeDtypeStruct((rows, width_k), BF16),
        ),
        in_specs=[smem, smem] + [vmem] * 6,
        out_specs=[vmem] * 3,
        scratch_shapes=[
            pltpu.VMEM((n, block, 2 * width_q), BF16),
            pltpu.VMEM((n, block, 2 * width_q), BF16),
            pltpu.VMEM((n, block, HEAD_SIZE), F32),
            pltpu.VMEM((n, block, HEAD_SIZE), F32),
            pltpu.VMEM((rows, width_k), BF16),
            pltpu.VMEM((rows, width_k), BF16),
            pltpu.VMEM((kv_heads, 2, rows, HEAD_SIZE), BF16),
            pltpu.VMEM((kv_heads, 2, rows, HEAD_SIZE), BF16),
            pltpu.VMEM((n, block, width_q), BF16),
            pltpu.VMEM((n, block, width_q), BF16),
            pltpu.VMEM((rows, n * block), BF16),
            pltpu.VMEM((HEAD_SIZE, rows), F32),
            pltpu.VMEM((rows, rows), F32),
            pltpu.VMEM((rows, rows), F32),
            pltpu.VMEM((rows, n * block), F32),
            pltpu.VMEM((HEAD_SIZE, n * block), F32),
            pltpu.VMEM((width_q, rows), F32),
            pltpu.VMEM((rows, width_q), F32),
            pltpu.VMEM((rows, width_k), F32),
            pltpu.VMEM((rows, width_k), F32),
            dma((n,)),
            dma((n,)),
            dma((n,)),
            dma((n,)),
            dma((2,)),
            dma((2,)),
            dma((kv_heads,)),
            dma((kv_heads,)),
            dma((n,)),
            dma((n,)),
        ],
        compiler_params=pltpu.CompilerParams(
            collective_id=0, has_side_effects=True, vmem_limit_bytes=56 * 1024 * 1024
        ),
    )(lengths, plan, query, output_gradient, key, value, lse.T, delta.T)


def solution(mesh):
    rows = P(("grp", "cp"), None)
    return jax.shard_map(
        on_device,
        mesh=mesh,
        in_specs=(rows,) * 6 + (P(), P(("grp", "cp"))),
        out_specs=(rows,) * 3,
        check_vma=False,
    )
```

time: 154 us -> 41.5 us (0.27)
  the two profiles are of different devices: /device:TPU:11 before, /device:TPU:23 now
where the time goes in v1:
time: 41.5 us; the launch traced here: 41.3 us
  Pallas kernels  36.5 us (88%)
  local copies, waits for them, and re-layouts  4.1 us (10%)
  between operations  0.65 us (2%)
    pallas_call x1, Pallas kernels, on_device(): pl.pallas_call(functools.partial(kernel, n, groups), out_shape=(jax.Shape...  36.5 us
    unnamed x7, local copies, waits for them, and re-layouts  4.1 us

profile of v1, /device:TPU:23, one launch (start us, length us, event | category | flops | bytes accessed | tf_op | source)
XLA Modules:
  0.0 41.3 jit_solution(11564064213879690296)
XLA Ops:
  0.6 36.5 %shard_map.103 = (bf16[256,2048]{1,0:T(8,128)(2,1)}, bf16[256,512]{1,0:T(8,128)(2,1)}, bf16[256,512]{1,0:T(8,128)(2,1)}) custom-call(s32[4]{0:T(128)} %lengths.1, s32[16]{0:T(128)} %plan.1, bf16[256,2048]{1,0:T(8,128)(2,1)} %q_ref.1, bf16[256,2048]{1,0:T(8,128)(2,1)} %do_ref.1, bf16[256,512]{1,0:T(8,128)(2,1)} %k_ref.1, bf16[256,512]{1,0:T(8,128)(2,1)} %v_ref.1, ...), custom_call_target="tpu_custom_call" | custom-call | tf_op jit(solution)/shard_map/pallas_call | solution.py:403
  37.1 0.0 copy-start.1
  37.2 2.3 %copy.14 = bf16[256,2048]{1,0:T(8,128)(2,1)} copy(bf16[256,2048]{1,0:T(8,128)(2,1)} %get-tuple-element.6) | data formatting | bytes 2097152
  39.5 0.0 copy-done.1
  39.5 0.0 copy-start
  39.5 0.7 %copy.15 = bf16[256,512]{1,0:T(8,128)(2,1)} copy(bf16[256,512]{1,0:T(8,128)(2,1)S(1)} %copy-done.1) | data formatting | bytes 524288
  40.2 0.3 copy-done
  40.5 0.7 %copy.16 = bf16[256,512]{1,0:T(8,128)(2,1)} copy(bf16[256,512]{1,0:T(8,128)(2,1)S(1)} %copy-done) | data formatting | bytes 524288
Async XLA Ops:
  37.1 2.4 %copy-start.1 = (bf16[256,512]{1,0:T(8,128)(2,1)S(1)}, bf16[256,512]{1,0:T(8,128)(2,1)}, u32[]{:S(2)}) copy-start(bf16[256,512]{1,0:T(8,128)(2,1)} %get-tuple-element.7) | copy-start | bytes 786436
  39.5 1.0 %copy-start = (bf16[256,512]{1,0:T(8,128)(2,1)S(1)}, bf16[256,512]{1,0:T(8,128)(2,1)}, u32[]{:S(2)}) copy-start(bf16[256,512]{1,0:T(8,128)(2,1)} %get-tuple-element.8) | copy-start | bytes 786436

commit v2 on v1

--- a/solution.py
+++ b/solution.py
@@ -44,15 +44,19 @@
     groups,
     lengths,
     plan,
-    q_ref,
-    do_ref,
-    k_ref,
-    v_ref,
+    q_hbm,
+    do_hbm,
+    k_hbm,
+    v_hbm,
     lse_ref,
     delta_ref,
     dq_ref,
     dk_ref,
     dv_ref,
+    q_ref,
+    do_ref,
+    k_ref,
+    v_ref,
     slot_out,
     slot_in,
     stat_out,
@@ -83,6 +87,7 @@
     back_recv,
     dqs_send,
     dqs_recv,
+    load_sem,
 ):
     grp = lax.axis_index("grp")
     me = lax.axis_index("cp")
@@ -104,6 +109,14 @@
     sends = jnp.maximum(me - 1, 0)
 
     barrier = pltpu.get_barrier_semaphore()
+    loads = [
+        pltpu.make_async_copy(source, target, load_sem.at[i])
+        for i, (source, target) in enumerate(
+            ((q_hbm, q_ref), (do_hbm, do_ref), (k_hbm, k_ref), (v_hbm, v_ref))
+        )
+    ]
+    for load in loads:
+        load.start()
 
     def greet(step, carry):
         peer = lax.rem(me + step, n)
@@ -152,7 +165,9 @@
     pick = jnp.where((slot_row == wanted) & (owner[:1] >= 0), 1.0, 0.0)
     pick_low = pick.astype(BF16)
     pick_t[...] = pick.T.astype(BF16)
+    loads[0].wait()
     slot_out[:, :, :width_q] = dot_nn(pick_low, q_ref[...]).astype(BF16).reshape(n, block, width_q)
+    loads[1].wait()
     slot_out[:, :, width_q:] = dot_nn(pick_low, do_ref[...]).astype(BF16).reshape(n, block, width_q)
     stat_out[...] = jnp.dot(
         pick, packed.T, preferred_element_type=F32, precision=lax.Precision.HIGHEST
@@ -185,10 +200,10 @@
     def kv_copies():
         return (
             pltpu.make_async_remote_copy(
-                k_ref, k_prev, kv_send.at[0], kv_recv.at[0], device_id=right, device_id_type=MESH
+                k_hbm, k_prev, kv_send.at[0], kv_recv.at[0], device_id=right, device_id_type=MESH
             ),
             pltpu.make_async_remote_copy(
-                v_ref, v_prev, kv_send.at[1], kv_recv.at[1], device_id=right, device_id_type=MESH
+                v_hbm, v_prev, kv_send.at[1], kv_recv.at[1], device_id=right, device_id_type=MESH
             ),
         )
 
@@ -273,6 +288,8 @@
         dv_acc[:, cols] = dv
         return carry
 
+    loads[2].wait()
+    loads[3].wait()
     lax.fori_loop(0, kv_heads, own, 0)
 
     @pl.when(shard > 0)
@@ -299,36 +316,60 @@
 
     lax.fori_loop(0, kv_heads, prev, 0)
 
-    def arrive(m, carry):
-        for copy in slot_copies(m, m):
+    half = 2 * block
+    lanes = per * half
+    lane_head = lax.broadcasted_iota(jnp.int32, (1, lanes), 1) // half
+    key_pos = base + lax.broadcasted_iota(jnp.int32, (rows, lanes), 0)
+
+    def batch(j, carry):
+        m = 2 * j
+
+        @pl.when(m >= me + 2)
+        def _():
+            for copy in slot_copies(m, m):
+                copy.wait_recv()
+
+        for copy in slot_copies(m + 1, m + 1):
             copy.wait_recv()
-        return carry
-
-    lax.fori_loop(me + 2, n, arrive, 0)
-
-    @pl.when(me + 2 < n)
-    def _():
-        routed_t[...] = stat_in[...].reshape(count, HEAD_SIZE).T
-        key_pos = base + lax.broadcasted_iota(jnp.int32, (rows, count), 0)
+        pair = pl.ds(m, 2)
+        stat = stat_in[pair].reshape(half, HEAD_SIZE)
+        routed_t[...] = jnp.concatenate([stat] * per, axis=0).T
         first = routed_t[pl.ds(2 * heads, 1), :]
         live = routed_t[pl.ds(2 * heads + 8, 1), :] > 0.5
         bias_in[...] = jnp.where((key_pos.astype(F32) >= first) & live, 0.0, -jnp.inf)
 
+        def row_of(first_row):
+            out = routed_t[pl.ds(first_row, 1), :]
+            for u in range(1, per):
+                out = jnp.where(lane_head == u, routed_t[pl.ds(first_row + u, 1), :], out)
+            return out
+
         def routed(g, carry):
             cols = columns(g)
             hs = [g * per + u for u in range(per)]
+
+            def stack(offset):
+                return jnp.concatenate(
+                    [
+                        slot_in[pair, :, columns(offset + h)].reshape(half, HEAD_SIZE)
+                        for h in hs
+                    ],
+                    axis=0,
+                )
+
             grad_query, dk, dv = group_grads(
-                [slot_in[:, :, columns(h)].reshape(count, HEAD_SIZE) for h in hs],
-                [slot_in[:, :, columns(heads + h)].reshape(count, HEAD_SIZE) for h in hs],
-                [routed_t[pl.ds(h, 1), :] for h in hs],
-                [routed_t[pl.ds(heads + h, 1), :] for h in hs],
+                [stack(0)],
+                [stack(heads)],
+                [row_of(g * per)],
+                [row_of(heads + g * per)],
                 k_ref[:, cols],
                 v_ref[:, cols],
                 bias_in[...],
             )
+            back = (grad_query[0] * FACTOR).T.astype(BF16)
             for u in range(per):
-                dq_out[:, :, columns(hs[u])] = (
-                    (grad_query[u] * FACTOR).T.astype(BF16).reshape(n, block, HEAD_SIZE)
+                dq_out[pair, :, columns(hs[u])] = back[u * half : (u + 1) * half].reshape(
+                    2, block, HEAD_SIZE
                 )
             dk_acc[:, cols] += dk
             dv_acc[:, cols] += dv
@@ -336,11 +377,14 @@
 
         lax.fori_loop(0, kv_heads, routed, 0)
 
-        def give_back(m, carry):
+        @pl.when(m >= me + 2)
+        def _():
             dq_copy(m, me).start()
-            return carry
-
-        lax.fori_loop(me + 2, n, give_back, 0)
+
+        dq_copy(m + 1, me).start()
+        return carry
+
+    lax.fori_loop((me + 2) // 2, n // 2, batch, 0)
 
     for g in range(kv_heads):
 
@@ -397,6 +441,7 @@
     width_k = key.shape[1]
     kv_heads = width_k // HEAD_SIZE
     block = rows // plan.shape[0]
+    lanes = 2 * block * (width_q // width_k)
     vmem = pl.BlockSpec(memory_space=pltpu.VMEM)
     smem = pl.BlockSpec(memory_space=pltpu.SMEM)
     dma = pltpu.SemaphoreType.DMA
@@ -407,9 +452,13 @@
             jax.ShapeDtypeStruct((rows, width_k), BF16),
             jax.ShapeDtypeStruct((rows, width_k), BF16),
         ),
-        in_specs=[smem, smem] + [vmem] * 6,
+        in_specs=[smem, smem] + [pl.BlockSpec(memory_space=pl.ANY)] * 4 + [vmem] * 2,
         out_specs=[vmem] * 3,
         scratch_shapes=[
+            pltpu.VMEM((rows, width_q), BF16),
+            pltpu.VMEM((rows, width_q), BF16),
+            pltpu.VMEM((rows, width_k), BF16),
+            pltpu.VMEM((rows, width_k), BF16),
             pltpu.VMEM((n, block, 2 * width_q), BF16),
             pltpu.VMEM((n, block, 2 * width_q), BF16),
             pltpu.VMEM((n, block, HEAD_SIZE), F32),
@@ -424,8 +473,8 @@
             pltpu.VMEM((HEAD_SIZE, rows), F32),
             pltpu.VMEM((rows, rows), F32),
             pltpu.VMEM((rows, rows), F32),
-            pltpu.VMEM((rows, n * block), F32),
-            pltpu.VMEM((HEAD_SIZE, n * block), F32),
+            pltpu.VMEM((rows, lanes), F32),
+            pltpu.VMEM((HEAD_SIZE, lanes), F32),
             pltpu.VMEM((width_q, rows), F32),
             pltpu.VMEM((rows, width_q), F32),
             pltpu.VMEM((rows, width_k), F32),
@@ -440,6 +489,7 @@
             dma((kv_heads,)),
             dma((n,)),
             dma((n,)),
+            dma((4,)),
         ],
         compiler_params=pltpu.CompilerParams(
             collective_id=0, has_side_effects=True, vmem_limit_bytes=56 * 1024 * 1024

time: 41.5 us -> 38.4 us (0.925)
  Pallas kernels: 36.5 us -> 33.4 us
    pallas_call x1, Pallas kernels: 36.5 us -> 33.4 us  [on_device(): pl.pallas_call(functools.partial(kernel, n, groups), out_shape=(jax.Shape...]
where the time goes in v2:
time: 38.4 us; the launch traced here: 38.2 us
  Pallas kernels  33.4 us (87%)
  local copies, waits for them, and re-layouts  4.1 us (11%)
  between operations  0.65 us (2%)
    pallas_call x1, Pallas kernels, on_device(): pl.pallas_call(functools.partial(kernel, n, groups), out_shape=(jax.Shape...  33.4 us
    unnamed x7, local copies, waits for them, and re-layouts  4.1 us

profile of v2, /device:TPU:23, one launch (start us, length us, event | category | flops | bytes accessed | tf_op | source)
XLA Modules:
  0.0 38.2 jit_solution(15224182406953981967)
XLA Ops:
  0.6 33.4 %shard_map.103 = (bf16[256,2048]{1,0:T(8,128)(2,1)}, bf16[256,512]{1,0:T(8,128)(2,1)}, bf16[256,512]{1,0:T(8,128)(2,1)}) custom-call(s32[4]{0:T(128)} %lengths.1, s32[16]{0:T(128)} %plan.1, bf16[256,2048]{1,0:T(8,128)(2,1)} %q_hbm.1, bf16[256,2048]{1,0:T(8,128)(2,1)} %do_hbm.1, bf16[256,512]{1,0:T(8,128)(2,1)} %k_hbm.1, bf16[256,512]{1,0:T(8,128)(2,1)} %v_hbm.1, ...), custom_call_target="tpu_custom_call" | custom-call | tf_op jit(solution)/shard_map/pallas_call | solution.py:448
  34.1 0.0 copy-start.1
  34.1 2.3 %copy.14 = bf16[256,2048]{1,0:T(8,128)(2,1)} copy(bf16[256,2048]{1,0:T(8,128)(2,1)} %get-tuple-element.6) | data formatting | bytes 2097152
  36.4 0.0 copy-done.1
  36.4 0.0 copy-start
  36.5 0.7 %copy.15 = bf16[256,512]{1,0:T(8,128)(2,1)} copy(bf16[256,512]{1,0:T(8,128)(2,1)S(1)} %copy-done.1) | data formatting | bytes 524288
  37.2 0.3 copy-done
  37.5 0.7 %copy.16 = bf16[256,512]{1,0:T(8,128)(2,1)} copy(bf16[256,512]{1,0:T(8,128)(2,1)S(1)} %copy-done) | data formatting | bytes 524288
Async XLA Ops:
  34.1 2.4 %copy-start.1 = (bf16[256,512]{1,0:T(8,128)(2,1)S(1)}, bf16[256,512]{1,0:T(8,128)(2,1)}, u32[]{:S(2)}) copy-start(bf16[256,512]{1,0:T(8,128)(2,1)} %get-tuple-element.7) | copy-start | bytes 786436
  36.4 1.0 %copy-start = (bf16[256,512]{1,0:T(8,128)(2,1)S(1)}, bf16[256,512]{1,0:T(8,128)(2,1)}, u32[]{:S(2)}) copy-start(bf16[256,512]{1,0:T(8,128)(2,1)} %get-tuple-element.8) | copy-start | bytes 786436

commit v3 on v2

--- a/solution.py
+++ b/solution.py
@@ -50,9 +50,10 @@
     v_hbm,
     lse_ref,
     delta_ref,
-    dq_ref,
-    dk_ref,
-    dv_ref,
+    dq_hbm,
+    dq_in_hbm,
+    dk_hbm,
+    dv_hbm,
     q_ref,
     do_ref,
     k_ref,
@@ -67,7 +68,6 @@
     back_in,
     dq_out,
     dq_in,
-    pick_t,
     stats_t,
     bias_own,
     bias_prev,
@@ -77,6 +77,8 @@
     dq_acc,
     dk_acc,
     dv_acc,
+    dk_ref,
+    dv_ref,
     slot_send,
     slot_recv,
     stat_send,
@@ -88,6 +90,7 @@
     dqs_send,
     dqs_recv,
     load_sem,
+    store_sem,
 ):
     grp = lax.axis_index("grp")
     me = lax.axis_index("cp")
@@ -164,7 +167,6 @@
     wanted = owner[:1] * block + within[:1]
     pick = jnp.where((slot_row == wanted) & (owner[:1] >= 0), 1.0, 0.0)
     pick_low = pick.astype(BF16)
-    pick_t[...] = pick.T.astype(BF16)
     loads[0].wait()
     slot_out[:, :, :width_q] = dot_nn(pick_low, q_ref[...]).astype(BF16).reshape(n, block, width_q)
     loads[1].wait()
@@ -304,7 +306,7 @@
         )
         for u in range(per):
             where = columns(g * per + u)
-            dq_acc[:, where] = ((dq_t[where, :] + grad_query[u]) * FACTOR).T
+            dq_acc[:, where] = ((dq_t[where, :] + grad_query[u]) * FACTOR).T.astype(BF16)
         back_out[g, 0] = (dk * FACTOR).astype(BF16)
         back_out[g, 1] = dv.astype(BF16)
 
@@ -315,6 +317,13 @@
         return carry
 
     lax.fori_loop(0, kv_heads, prev, 0)
+    stores = [
+        pltpu.make_async_copy(source, target, store_sem.at[i])
+        for i, (source, target) in enumerate(
+            ((dq_acc, dq_hbm), (dk_ref, dk_hbm), (dv_ref, dv_hbm), (dq_in, dq_in_hbm))
+        )
+    ]
+    stores[0].start()
 
     half = 2 * block
     lanes = per * half
@@ -396,19 +405,15 @@
         dk_ref[:, cols] = (dk_acc[:, cols] * FACTOR + back_in[g, 0].astype(F32)).astype(BF16)
         dv_ref[:, cols] = (dv_acc[:, cols] + back_in[g, 1].astype(F32)).astype(BF16)
 
+    stores[1].start()
+    stores[2].start()
+
     def take(p, carry):
         dq_copy(p, p).wait_recv()
         return carry
 
     lax.fori_loop(0, sends, take, 0)
-
-    def finish(h, carry):
-        cols = columns(h)
-        extra = dot_nn(pick_t[...], dq_in[:, :, cols].reshape(count, HEAD_SIZE))
-        dq_ref[:, cols] = (dq_acc[:, cols] + extra).astype(BF16)
-        return carry
-
-    lax.fori_loop(0, heads, finish, 0)
+    stores[3].start()
 
     @pl.when(shard < last)
     def _():
@@ -432,6 +437,22 @@
         return carry
 
     lax.fori_loop(me + 2, n, sent_back, 0)
+    for store in stores:
+        store.wait()
+
+
+def finish(plan, dq_near, dq_far, dk, dv, dq_ref, dk_ref, dv_ref):
+    block = dq_far.shape[1]
+    blocks = dq_near.shape[0] // block
+    first = pl.program_id(0) * blocks
+    for b in range(blocks):
+        owner = plan[first + b]
+        at = pl.ds(b * block, block)
+        near = dq_near[at, :].astype(F32)
+        far = dq_far[jnp.maximum(owner, 0)].astype(F32)
+        dq_ref[at, :] = jnp.where(owner >= 0, near + far, near).astype(BF16)
+    dk_ref[...] = dk[...]
+    dv_ref[...] = dv[...]
 
 
 def on_device(query, key, value, output_gradient, lse, delta, lengths, plan):
@@ -445,15 +466,17 @@
     vmem = pl.BlockSpec(memory_space=pltpu.VMEM)
     smem = pl.BlockSpec(memory_space=pltpu.SMEM)
     dma = pltpu.SemaphoreType.DMA
-    return pl.pallas_call(
+    anywhere = pl.BlockSpec(memory_space=pl.ANY)
+    parts = pl.pallas_call(
         functools.partial(kernel, n, groups),
         out_shape=(
             jax.ShapeDtypeStruct((rows, width_q), BF16),
+            jax.ShapeDtypeStruct((n, block, width_q), BF16),
             jax.ShapeDtypeStruct((rows, width_k), BF16),
             jax.ShapeDtypeStruct((rows, width_k), BF16),
         ),
-        in_specs=[smem, smem] + [pl.BlockSpec(memory_space=pl.ANY)] * 4 + [vmem] * 2,
-        out_specs=[vmem] * 3,
+        in_specs=[smem, smem] + [anywhere] * 4 + [vmem] * 2,
+        out_specs=[anywhere] * 4,
         scratch_shapes=[
             pltpu.VMEM((rows, width_q), BF16),
             pltpu.VMEM((rows, width_q), BF16),
@@ -469,16 +492,17 @@
             pltpu.VMEM((kv_heads, 2, rows, HEAD_SIZE), BF16),
             pltpu.VMEM((n, block, width_q), BF16),
             pltpu.VMEM((n, block, width_q), BF16),
-            pltpu.VMEM((rows, n * block), BF16),
             pltpu.VMEM((HEAD_SIZE, rows), F32),
             pltpu.VMEM((rows, rows), F32),
             pltpu.VMEM((rows, rows), F32),
             pltpu.VMEM((rows, lanes), F32),
             pltpu.VMEM((HEAD_SIZE, lanes), F32),
             pltpu.VMEM((width_q, rows), F32),
-            pltpu.VMEM((rows, width_q), F32),
+            pltpu.VMEM((rows, width_q), BF16),
             pltpu.VMEM((rows, width_k), F32),
             pltpu.VMEM((rows, width_k), F32),
+            pltpu.VMEM((rows, width_k), BF16),
+            pltpu.VMEM((rows, width_k), BF16),
             dma((n,)),
             dma((n,)),
             dma((n,)),
@@ -490,11 +514,30 @@
             dma((n,)),
             dma((n,)),
             dma((4,)),
+            dma((4,)),
         ],
         compiler_params=pltpu.CompilerParams(
             collective_id=0, has_side_effects=True, vmem_limit_bytes=56 * 1024 * 1024
         ),
     )(lengths, plan, query, output_gradient, key, value, lse.T, delta.T)
+    steps = 4
+    wide = pl.BlockSpec((rows // steps, width_q), lambda i, plan: (i, 0))
+    narrow = pl.BlockSpec((rows // steps, width_k), lambda i, plan: (i, 0))
+    whole = pl.BlockSpec((n, block, width_q), lambda i, plan: (0, 0, 0))
+    return pl.pallas_call(
+        finish,
+        out_shape=(
+            jax.ShapeDtypeStruct((rows, width_q), BF16),
+            jax.ShapeDtypeStruct((rows, width_k), BF16),
+            jax.ShapeDtypeStruct((rows, width_k), BF16),
+        ),
+        grid_spec=pltpu.PrefetchScalarGridSpec(
+            num_scalar_prefetch=1,
+            grid=(steps,),
+            in_specs=[wide, whole, narrow, narrow],
+            out_specs=[wide, narrow, narrow],
+        ),
+    )(plan, *parts)
 
 
 def solution(mesh):

time: 38.4 us -> 36 us (0.938)
  local copies, waits for them, and re-layouts: 4.1 us -> 0 us
  Pallas kernels: 33.4 us -> 35.1 us
    pallas_call x0 -> x1, Pallas kernels: none -> 4.59 us  [on_device(): pl.pallas_call(finish, out_shape=(jax.ShapeDtypeStruct((rows, width_q), B...]
    unnamed x7 -> x0, local copies, waits for them, and re-layouts: 4.1 us -> none
    pallas_call x1, Pallas kernels: 33.4 us -> 30.6 us  [on_device(): pl.pallas_call(functools.partial(kernel, n, groups), out_shape=(jax.Shape...]
where the time goes in v3:
time: 36 us; the launch traced here: 35.8 us
  Pallas kernels  35.1 us (98%)
  between operations  0.64 us (2%)
    pallas_call x1, Pallas kernels, on_device(): pl.pallas_call(functools.partial(kernel, n, groups), out_shape=(jax.Shape...  30.6 us
    pallas_call x1, Pallas kernels, on_device(): pl.pallas_call(finish, out_shape=(jax.ShapeDtypeStruct((rows, width_q), B...  4.59 us

profile of v3, /device:TPU:23, one launch (start us, length us, event | category | flops | bytes accessed | tf_op | source)
XLA Modules:
  0.0 35.8 jit_solution(12035560724587525871)
XLA Ops:
  0.6 30.6 %shard_map.103 = (bf16[256,2048]{1,0:T(8,128)(2,1)}, bf16[8,16,2048]{2,1,0:T(8,128)(2,1)}, bf16[256,512]{1,0:T(8,128)(2,1)}, bf16[256,512]{1,0:T(8,128)(2,1)}) custom-call(s32[4]{0:T(128)} %lengths.1, s32[16]{0:T(128)} %plan.3, bf16[256,2048]{1,0:T(8,128)(2,1)} %q_hbm.1, bf16[256,2048]{1,0:T(8,128)(2,1)} %do_hbm.1, bf16[256,512]{1,0:T(8,128)(2,1)} %k_hbm.1, ...), custom_call_target="tpu_custom_call" | custom-call | tf_op jit(solution)/shard_map/pallas_call | solution.py:470
  31.2 4.6 %shard_map.104 = (bf16[256,2048]{1,0:T(8,128)(2,1)}, bf16[256,512]{1,0:T(8,128)(2,1)}, bf16[256,512]{1,0:T(8,128)(2,1)}) custom-call(s32[16]{0:T(128)} %plan.3, bf16[256,2048]{1,0:T(8,128)(2,1)} %get-tuple-element.7.dq_near, bf16[8,16,2048]{2,1,0:T(8,128)(2,1)} %get-tuple-element.8.dq_far, bf16[256,512]{1,0:T(8,128)(2,1)} %get-tuple-element.9.dk, ...), custom_call_target="tpu_custom_call" | custom-call | tf_op jit(solution)/shard_map/pallas_call | solution.py:527

commit v4 on v3

--- a/solution.py
+++ b/solution.py
@@ -331,7 +331,7 @@
     key_pos = base + lax.broadcasted_iota(jnp.int32, (rows, lanes), 0)
 
     def batch(j, carry):
-        m = 2 * j
+        m = n - 2 - 2 * j
 
         @pl.when(m >= me + 2)
         def _():
@@ -393,7 +393,7 @@
         dq_copy(m + 1, me).start()
         return carry
 
-    lax.fori_loop((me + 2) // 2, n // 2, batch, 0)
+    lax.fori_loop(0, n // 2 - (me + 2) // 2, batch, 0)
 
     for g in range(kv_heads):
 
@@ -520,7 +520,7 @@
             collective_id=0, has_side_effects=True, vmem_limit_bytes=56 * 1024 * 1024
         ),
     )(lengths, plan, query, output_gradient, key, value, lse.T, delta.T)
-    steps = 4
+    steps = 2
     wide = pl.BlockSpec((rows // steps, width_q), lambda i, plan: (i, 0))
     narrow = pl.BlockSpec((rows // steps, width_k), lambda i, plan: (i, 0))
     whole = pl.BlockSpec((n, block, width_q), lambda i, plan: (0, 0, 0))

time: 36 us -> 34 us (0.944)
  the two profiles are of different devices: /device:TPU:23 before, /device:TPU:27 now
where the time goes in v4:
time: 34 us; the launch traced here: 33.8 us
  Pallas kernels  33.2 us (98%)
  between operations  0.64 us (2%)
    pallas_call x1, Pallas kernels, on_device(): pl.pallas_call(functools.partial(kernel, n, groups), out_shape=(jax.Shape...  29.9 us
    pallas_call x1, Pallas kernels, on_device(): pl.pallas_call(finish, out_shape=(jax.ShapeDtypeStruct((rows, width_q), B...  3.26 us

profile of v4, /device:TPU:27, one launch (start us, length us, event | category | flops | bytes accessed | tf_op | source)
XLA Modules:
  0.0 33.8 jit_solution(8222593025501424183)
XLA Ops:
  0.6 29.9 %shard_map.103 = (bf16[256,2048]{1,0:T(8,128)(2,1)}, bf16[8,16,2048]{2,1,0:T(8,128)(2,1)}, bf16[256,512]{1,0:T(8,128)(2,1)}, bf16[256,512]{1,0:T(8,128)(2,1)}) custom-call(s32[4]{0:T(128)} %lengths.1, s32[16]{0:T(128)} %plan.3, bf16[256,2048]{1,0:T(8,128)(2,1)} %q_hbm.1, bf16[256,2048]{1,0:T(8,128)(2,1)} %do_hbm.1, bf16[256,512]{1,0:T(8,128)(2,1)} %k_hbm.1, ...), custom_call_target="tpu_custom_call" | custom-call | tf_op jit(solution)/shard_map/pallas_call | solution.py:470
  30.5 3.3 %shard_map.104 = (bf16[256,2048]{1,0:T(8,128)(2,1)}, bf16[256,512]{1,0:T(8,128)(2,1)}, bf16[256,512]{1,0:T(8,128)(2,1)}) custom-call(s32[16]{0:T(128)} %plan.3, bf16[256,2048]{1,0:T(8,128)(2,1)} %get-tuple-element.7.dq_near, bf16[8,16,2048]{2,1,0:T(8,128)(2,1)} %get-tuple-element.8.dq_far, bf16[256,512]{1,0:T(8,128)(2,1)} %get-tuple-element.9.dk, ...), custom_call_target="tpu_custom_call" | custom-call | tf_op jit(solution)/shard_map/pallas_call | solution.py:527
